TPU v7x, 128 devices: a whole 4x4x4 slice. The times are simulated.
128 devices in a mesh: gx: 8 (over y_lo, z), gy: 16 (over y_hi, x, core).
Axes of the slice: x: 4, y: 4 (y_hi: 2, y_lo: 2; y = y_hi * 2 + y_lo), z: 4, core: 2. Of those that a mesh axis runs over, the one named last changes fastest.
Arguments:
- features: bfloat16 [64, 256, 16, 128], P('gx', 'gy'), may hold values from -6 to 6
- w_first: bfloat16 [27, 128, 128], replicated, may hold values from -0.109375 to 0.109375
- w_second: bfloat16 [27, 128, 128], replicated, may hold values from -0.109375 to 0.109375
- occupancy: int32 [8, 32, 2], P('gx', 'gy'), may hold values from 0 to 1, as said below
- cotangent: bfloat16 [64, 256, 16, 128], P('gx', 'gy'), may hold values from -6 to 6
Outputs:
- output: bfloat16 [64, 256, 16, 128], P('gx', 'gy')
- grad_features: bfloat16 [64, 256, 16, 128], P('gx', 'gy')
- grad_first: float32 [27, 128, 128], P(None, 'gy')
- grad_second: float32 [27, 128, 128], P(None, 'gy')
Inputs may be any that keep to these rules, and one draw needn't show every extreme that they name: `occupancy`: 1 marks an active block; the share of active blocks differs from one tile of 1 x 2 x 2 blocks to another.
All inputs are finite; a program needn't handle non-finite values.
Results may differ from a plain program's by a relative error of at most 0.0025.
The roundings to bfloat16 on the way count: a program that leaves them out, or rounds other values in their place, can miss the bound.
Values may be sent and summed in bfloat16 or wider, within the bound.
A program may use at most 128 MiB of HBM per device.

v0:
```python
import functools
import math

import jax
import jax.numpy as jnp
from jax import lax
from jax.experimental import pallas as pl
from jax.experimental.pallas import tpu as pltpu
from jax.sharding import PartitionSpec as P

F32 = jnp.float32
BF16 = jnp.bfloat16
MESH = pl.DeviceIdType.MESH
DIRS = [(ax, ay) for ax in (-1, 0, 1) for ay in (-1, 0, 1) if (ax, ay) != (0, 0)]
GX, GY = 8, 16
X, Y, Z, C = 8, 16, 16, 128
TAPS = 28
ALL = [(0, 8, 0, 8)]
INNER = [(1, 6, 1, 6)]
RIM = [(0, 1, 0, 8), (7, 1, 0, 8), (1, 6, 0, 1), (1, 6, 7, 1)]


def kernel(
    scale,
    occ_ref, feat_hbm, cot_hbm, w1_hbm, w2_hbm,
    out_hbm, gf_hbm, g1_hbm, g2_hbm,
    feat, cot, w1, w2, fu, hq, slope, at, outs, part,
    r0, s0, r1a, r1b, r1c, a1, b1, c1, r2a, r2b, r2c, ab2, c2, r3, r3c, ab3, c3, r4, rc4, done,
    in_sem, out_sem, hs, hr, s0s, s0r, s1s, s1r, s2s, s2r, s3s, s3r, s4s, s4r,
):
    gx = lax.axis_index("gx")
    gy = lax.axis_index("gy")
    core = gy % 2
    px = (gy // 2) % 4
    yh = gy // 8
    pz = gx % 4
    yl = gx // 4
    py = yh * 2 + yl

    def at_x(k):
        return (px + k) % 4

    def at_y(k):
        return (py + k) % 4

    def at_z(k):
        return (pz + k) % 4

    def dev_x(k):
        return (gx, yh * 8 + at_x(k) * 2 + core)

    def dev_y(k):
        to = at_y(k)
        return ((to % 2) * 4 + pz, (to // 2) * 8 + px * 2 + core)

    def dev_z(k):
        return (yl * 4 + at_z(k), gy)

    partner = (gx, gy + 1 - 2 * core)

    def exists(ax, ay):
        ok = None
        for step, pos, size in ((ax, gx, GX), (ay, gy, GY)):
            if step == 0:
                continue
            here = pos + 1 < size if step > 0 else pos > 0
            ok = here if ok is None else jnp.logical_and(ok, here)
        return ok

    barrier = pltpu.get_barrier_semaphore()
    for ax, ay in DIRS:
        @pl.when(exists(ax, ay))
        def _():
            pl.semaphore_signal(barrier, inc=1, device_id=(gx + ax, gy + ay), device_id_type=MESH)
    fixed = [partner] + [dev_x(k) for k in (1, 2, 3)] + [dev_y(k) for k in (1, 2, 3)]
    fixed += [((gx + k) % GX, gy) for k in range(1, GX)]
    for peer in fixed:
        pl.semaphore_signal(barrier, inc=1, device_id=peer, device_id_type=MESH)

    loads = [
        pltpu.make_async_copy(src, dst, in_sem.at[i])
        for i, (src, dst) in enumerate(
            ((feat_hbm, feat), (cot_hbm, cot), (w1_hbm, w1), (w2_hbm, w2))
        )
    ]
    for load in loads:
        load.start()

    low = lax.broadcasted_iota(jnp.int32, (Z, C), 0) < 8
    mask = [
        jnp.where(low, occ_ref[0, b, 0].astype(F32), occ_ref[0, b, 1].astype(F32)) for b in range(2)
    ]

    def mask_rows(boxes, wide):
        rows = []
        for x0, nx, k0, nk in boxes:
            for _ in range(nx):
                rows += [mask[k // 4] for k in range(k0, k0 + nk)]
        m = jnp.concatenate(rows, axis=0)
        return jnp.concatenate([m, m], axis=1) if wide else m

    def z_shift(field, at_index):
        v = field[(1, *at_index)].astype(F32)
        n = math.prod(v.shape[:-1])
        t = v.reshape(n, C)
        z = lax.broadcasted_iota(jnp.int32, (n, C), 0) % Z
        down = jnp.where(z == 0, 0.0, pltpu.roll(t, 1, 0))
        up = jnp.where(z == Z - 1, 0.0, pltpu.roll(t, n - 1, 0))
        field[(0, *at_index)] = down.astype(BF16).reshape(v.shape)
        field[(2, *at_index)] = up.astype(BF16).reshape(v.shape)

    def edge_x(step, recv):
        if step == 0:
            return (pl.ds(1, X),)
        if recv:
            return (0 if step > 0 else X + 1,)
        return (X if step > 0 else 1,)

    def edge_y(step, recv):
        if step == 0:
            return (pl.ds(1, 8),)
        if recv:
            return (0, 1) if step > 0 else (9, 0)
        return (8, 1) if step > 0 else (1, 0)

    def halo_copy(ref, d, slot):
        ax, ay = DIRS[d]
        lead = (1,) if len(ref.shape) == 6 else (slice(None), 1)
        return pltpu.make_async_remote_copy(
            src_ref=ref.at[(*lead, *edge_x(ax, False), *edge_y(ay, False))],
            dst_ref=ref.at[(*lead, *edge_x(ax, True), *edge_y(ay, True))],
            send_sem=hs.at[slot, d],
            recv_sem=hr.at[slot, d],
            device_id=(gx + ax, gy + ay),
            device_id_type=MESH,
        )

    def halo_start(ref, slot):
        for d, (ax, ay) in enumerate(DIRS):
            @pl.when(exists(ax, ay))
            def _():
                halo_copy(ref, d, slot).start()

    def halo_zero(ref):
        lead = (1,) if len(ref.shape) == 6 else (slice(None), 1)
        for ax, ay in DIRS:
            @pl.when(jnp.logical_not(exists(-ax, -ay)))
            def _():
                index = (*lead, *edge_x(ax, True), *edge_y(ay, True))
                ref[index] = jnp.zeros(ref.at[index].shape, BF16)

    def halo_wait(ref, slot):
        for d, (ax, ay) in enumerate(DIRS):
            @pl.when(exists(-ax, -ay))
            def _():
                halo_copy(ref, d, slot).wait_recv()

    def halo_sent(ref, slot):
        for d, (ax, ay) in enumerate(DIRS):
            @pl.when(exists(ax, ay))
            def _():
                halo_copy(ref, d, slot).wait_send()

    def shift_rim(field):
        for x in (0, X + 1):
            z_shift(field, (x,))
        for edge in ((0, 1), (9, 0)):
            z_shift(field, (pl.ds(1, X), *edge))

    def shift_inner(field):
        for x in range(1, X + 1):
            z_shift(field, (x, pl.ds(1, 8)))

    def rows_of(field, boxes, dz, dx, j):
        halves = []
        for h in range(2):
            pieces = [
                field[dz, pl.ds(x0 + dx, nx), pl.ds(k0 + j + h, nk), 1 - h].reshape(nx * nk * Z, C)
                for x0, nx, k0, nk in boxes
            ]
            halves.append(jnp.concatenate(pieces, axis=0) if len(pieces) > 1 else pieces[0])
        return jnp.concatenate(halves, axis=1)

    zero = jnp.zeros((C, C), BF16)

    def conv(field, w, boxes, flipped):
        left, right = [], []
        for dx in range(3):
            for dz in range(3):
                tap = [w[26 - (9 * dx + 3 * dy + dz)] if flipped else w[9 * dx + 3 * dy + dz] for dy in range(3)]
                for j in range(2):
                    left.append(rows_of(field, boxes, dz, dx, j))
                    if j == 0:
                        grid = ((tap[0], zero), (tap[1], tap[0]))
                    else:
                        grid = ((tap[2], tap[1]), (zero, tap[2]))
                    if flipped:
                        grid = tuple(zip(*grid))
                        right.append(jnp.concatenate([jnp.concatenate(r, axis=1) for r in grid], axis=0))
                    else:
                        right.append(jnp.concatenate([jnp.concatenate(r, axis=1) for r in grid], axis=0))
        lhs = jnp.concatenate(left, axis=1)
        if flipped:
            return lax.dot_general(
                lhs, jnp.concatenate(right, axis=1), (((1,), (1,)), ((), ())), preferred_element_type=F32
            )
        return jnp.dot(lhs, jnp.concatenate(right, axis=0), preferred_element_type=F32)

    def tiles(boxes):
        at_row = 0
        for x0, nx, k0, nk in boxes:
            n = nx * nk * Z
            yield (x0, nx, k0, nk), slice(at_row, at_row + n)
            at_row += n

    def put(field_at, boxes, value):
        for (x0, nx, k0, nk), rows in tiles(boxes):
            for h in range(2):
                field_at(x0, nx, k0, nk, h, value[rows, h * C : (h + 1) * C].reshape(nx, nk, Z, C))

    def put_padded(field):
        def store(x0, nx, k0, nk, h, v):
            field[1, pl.ds(x0 + 1, nx), pl.ds(k0 + 1, nk), h] = v.astype(BF16)
        return store

    def forward(boxes):
        pre = conv(fu.at[0], w1, boxes, False)
        s = jax.nn.sigmoid(pre)
        m = mask_rows(boxes, True)
        put(put_padded(hq.at[0]), boxes, m * (pre * s))
        d = m * (s * (1.0 + pre * (1.0 - s)))
        for (x0, nx, k0, nk), rows in tiles(boxes):
            slope[pl.ds(x0, nx), pl.ds(k0, nk)] = d[rows].reshape(nx, nk, Z, 2 * C)

    def backward(boxes):
        grad = conv(fu.at[1], w2, boxes, True)
        d = [slope[pl.ds(x0, nx), pl.ds(k0, nk)].reshape(nx * nk * Z, 2 * C) for x0, nx, k0, nk in boxes]
        d = jnp.concatenate(d, axis=0) if len(d) > 1 else d[0]
        put(put_padded(hq.at[1]), boxes, grad * d)

    def finish(slot, w, flipped, boxes):
        acc = conv(hq.at[slot], w, boxes, flipped) * mask_rows(boxes, True)
        base = fu.at[slot]

        def store(x0, nx, k0, nk, h, v):
            b = base[1, pl.ds(x0 + 1, nx), pl.ds(k0 + 1, nk), h].astype(F32)
            outs[slot, pl.ds(x0, nx), pl.ds(k0, nk), h] = (b + v).astype(BF16)
        put(store, boxes, acc)

    def wgrad(g, left, right, mirrored):
        for h in range(2):
            for x in range(X):
                at[h, x] = left[1, x + 1, pl.ds(1, 8), h].reshape(8 * Z, C).T
        lhs = jnp.concatenate([at[h, x] for h in range(2) for x in range(X)], axis=1)

        @pl.loop(0, 3)
        def _(dx):
            cols = []
            for t in range(9):
                dy, dz = t // 3, t % 3
                ex, ey, ez = (2 - dx, 2 - dy, 2 - dz) if mirrored else (dx, dy, dz)
                halves = []
                for h in range(2):
                    row = h + ey + 1
                    halves.append(right[ez, pl.ds(ex, X), pl.ds(row // 2, 8), row % 2].reshape(X * 8 * Z, C))
                cols.append(jnp.concatenate(halves, axis=0))
            rhs = jnp.concatenate(cols, axis=1)
            acc = jnp.dot(lhs, rhs, preferred_element_type=F32)
            for t in range(9):
                block = acc[:, t * C : (t + 1) * C]
                if not mirrored:
                    block = block.T
                for s in range(16):
                    part[g, s % 2, (s // 2) % 4, s // 8, 9 * dx + t] = block[8 * s : 8 * s + 8]

    def remote(src, dst, send, recv, to):
        return pltpu.make_async_remote_copy(
            src_ref=src, dst_ref=dst, send_sem=send, recv_sem=recv, device_id=to, device_id_type=MESH
        )

    def stage0(g):
        return [remote(part.at[g, 1 - core], r0.at[g], s0s.at[g], s0r.at[g], partner)]

    def stage1(g):
        copies = []
        for k in (1, 2, 3):
            to = at_y(k)
            three = (
                (s0.at[g, at_x(k), :, pl.ds(0, 10)], r1a.at[g, k - 1], dev_x(k)),
                (s0.at[g, :, to // 2, pl.ds(10 + 5 * (to % 2), 5)], r1b.at[g, k - 1], dev_y(k)),
                (s0.at[g, :, :, pl.ds(20 + 2 * at_z(k), 2)], r1c.at[g, k - 1], dev_z(k)),
            )
            for i, (src, dst, dev) in enumerate(three):
                copies.append(remote(src, dst, s1s.at[g, i, k - 1], s1r.at[g, i, k - 1], dev))
        return copies

    def stage2(g):
        copies = []
        for k in (1, 2, 3):
            to = at_y(k)
            three = (
                (a1.at[g, to // 2, pl.ds(5 * (to % 2), 5)], r2a.at[g, k - 1], dev_y(k)),
                (b1.at[g, at_x(k)], r2b.at[g, k - 1], dev_x(k)),
                (c1.at[g, at_x(k)], r2c.at[g, k - 1], dev_x(k)),
            )
            for i, (src, dst, dev) in enumerate(three):
                copies.append(remote(src, dst, s2s.at[g, i, k - 1], s2r.at[g, i, k - 1], dev))
        return copies

    def stage3(g):
        copies = []
        for k in (1, 2, 3):
            to = at_y(k)
            two = (
                (ab2.at[g], r3.at[g, k - 1], dev_z(k)),
                (c2.at[g, to // 2, to % 2], r3c.at[g, k - 1], dev_y(k)),
            )
            for i, (src, dst, dev) in enumerate(two):
                copies.append(remote(src, dst, s3s.at[g, i, k - 1], s3r.at[g, i, k - 1], dev))
        return copies

    def stage4(g):
        copies = [remote(ab3.at[g], r4.at[g], s4s.at[g, 0], s4r.at[g, 0], ((gx + 4) % GX, gy))]
        for k in range(1, GX):
            copies.append(
                remote(c3.at[g], rc4.at[g, k - 1], s4s.at[g, k], s4r.at[g, k], ((gx + k) % GX, gy))
            )
        return copies

    def start(copies):
        for copy in copies:
            copy.start()

    def arrive(copies):
        for copy in copies:
            copy.wait_recv()

    def sum0(g):
        for i in range(4):
            s0[g, i] = part[g, core, i] + r0[g, i]

    def sum1(g):
        a1[g] = (s0[g, px, :, pl.ds(0, 10)] + r1a[g, 0]) + (r1a[g, 1] + r1a[g, 2])
        b1[g] = (s0[g, :, yh, pl.ds(10 + 5 * yl, 5)] + r1b[g, 0]) + (r1b[g, 1] + r1b[g, 2])
        c1[g] = (s0[g, :, :, pl.ds(20 + 2 * pz, 2)] + r1c[g, 0]) + (r1c[g, 1] + r1c[g, 2])

    def sum2(g):
        ab2[g, 0] = (a1[g, yh, pl.ds(5 * yl, 5)] + r2a[g, 0]) + (r2a[g, 1] + r2a[g, 2])
        ab2[g, 1] = (b1[g, px] + r2b[g, 0]) + (r2b[g, 1] + r2b[g, 2])
        c2[g] = (c1[g, px] + r2c[g, 0]) + (r2c[g, 1] + r2c[g, 2])

    def sum3(g):
        ab3[g] = (ab2[g] + r3[g, 0]) + (r3[g, 1] + r3[g, 2])
        c3[g] = (c2[g, yh, yl] + r3c[g, 0]) + (r3c[g, 1] + r3c[g, 2])

    def sum4(g):
        for i in range(2):
            done[g, pl.ds(10 * i + 5 * yl, 5)] = ab3[g, i] * scale
            done[g, pl.ds(10 * i + 5 * (1 - yl), 5)] = r4[g, i] * scale
        done[g, 20 + 2 * pz + yl] = c3[g] * scale
        for k in range(1, GX):
            source = (gx + GX - k) % GX
            done[g, 20 + 2 * (source % 4) + source // 4] = rc4[g, k - 1] * scale

    for g in range(2):
        part[g, :, :, :, 27] = jnp.zeros((2, 4, 2, 8, C), F32)

    for f, raw in enumerate((feat, cot)):
        loads[f].wait()
        for x in range(X):
            for b in range(2):
                rows = raw[x, pl.ds(4 * b, 4)].astype(F32) * mask[b][None, None]
                fu[f, 1, x + 1, pl.ds(4 * b + 1, 4)] = rows.astype(BF16)
    halo_zero(fu)
    halo_zero(hq)

    wide_x = 1 + (gx > 0).astype(jnp.int32) + (gx < GX - 1).astype(jnp.int32)
    wide_y = 1 + (gy > 0).astype(jnp.int32) + (gy < GY - 1).astype(jnp.int32)
    pl.semaphore_wait(barrier, len(fixed) + wide_x * wide_y - 1)

    halo_start(fu, 0)
    for f in range(2):
        shift_inner(fu.at[f])
    loads[2].wait()
    loads[3].wait()
    forward(INNER)
    backward(INNER)
    halo_wait(fu, 0)
    for f in range(2):
        shift_rim(fu.at[f])
    forward(RIM)
    halo_start(hq.at[0], 1)
    wgrad(1, hq.at[0], fu.at[1], True)
    start(stage0(1))
    backward(RIM)
    halo_start(hq.at[1], 2)
    shift_inner(hq.at[0])
    shift_inner(hq.at[1])
    arrive(stage0(1))
    sum0(1)
    start(stage1(1))
    wgrad(0, hq.at[1], fu.at[0], False)
    start(stage0(0))
    halo_wait(hq.at[0], 1)
    shift_rim(hq.at[0])
    arrive(stage1(1))
    sum1(1)
    start(stage2(1))
    arrive(stage0(0))
    sum0(0)
    start(stage1(0))
    finish(0, w2, False, ALL)
    out_copy = pltpu.make_async_copy(outs.at[0], out_hbm, out_sem.at[0])
    out_copy.start()
    halo_wait(hq.at[1], 2)
    shift_rim(hq.at[1])
    arrive(stage2(1))
    sum2(1)
    start(stage3(1))
    finish(1, w1, True, ALL)
    gf_copy = pltpu.make_async_copy(outs.at[1], gf_hbm, out_sem.at[1])
    gf_copy.start()
    arrive(stage3(1))
    sum3(1)
    start(stage4(1))
    arrive(stage1(0))
    sum1(0)
    start(stage2(0))
    arrive(stage2(0))
    sum2(0)
    start(stage3(0))
    arrive(stage4(1))
    sum4(1)
    g2_copy = pltpu.make_async_copy(done.at[1, pl.ds(0, 27)], g2_hbm, out_sem.at[2])
    g2_copy.start()
    arrive(stage3(0))
    sum3(0)
    start(stage4(0))
    arrive(stage4(0))
    sum4(0)
    g1_copy = pltpu.make_async_copy(done.at[0, pl.ds(0, 27)], g1_hbm, out_sem.at[3])
    g1_copy.start()

    halo_sent(fu, 0)
    halo_sent(hq.at[0], 1)
    halo_sent(hq.at[1], 2)
    for g in range(2):
        for stage in (stage0, stage1, stage2, stage3, stage4):
            for copy in stage(g):
                copy.wait_send()
    for copy in (out_copy, gf_copy, g2_copy, g1_copy):
        copy.wait()


def body(features, w_first, w_second, occupancy, cotangent):
    scale = 1.0 / math.sqrt(GX * GY * X * Y * Z)
    anyspace = pl.BlockSpec(memory_space=pl.ANY)
    dma = pltpu.SemaphoreType.DMA
    vm = pltpu.VMEM
    tile = (8, C)
    split = (X, 8, 2, Z, C)
    out, grad, first, second = pl.pallas_call(
        functools.partial(kernel, scale),
        name="section",
        out_shape=(
            jax.ShapeDtypeStruct((X, 8, 2, Z, C), BF16),
            jax.ShapeDtypeStruct((X, 8, 2, Z, C), BF16),
            jax.ShapeDtypeStruct((27, 8, C), F32),
            jax.ShapeDtypeStruct((27, 8, C), F32),
        ),
        in_specs=[pl.BlockSpec(memory_space=pltpu.SMEM)] + [anyspace] * 4,
        out_specs=(anyspace,) * 4,
        scratch_shapes=[
            vm((X, 8, 2, Z, C), BF16),
            vm((X, 8, 2, Z, C), BF16),
            vm((27, C, C), BF16),
            vm((27, C, C), BF16),
            vm((2, 3, X + 2, 10, 2, Z, C), BF16),
            vm((2, 3, X + 2, 10, 2, Z, C), BF16),
            vm((X, 8, Z, 2 * C), F32),
            vm((2, X, C, 8 * Z), BF16),
            vm((2, X, 8, 2, Z, C), BF16),
            vm((2, 2, 4, 2, TAPS, *tile), F32),
            vm((2, 4, 2, TAPS, *tile), F32),
            vm((2, 4, 2, TAPS, *tile), F32),
            vm((2, 3, 2, 10, *tile), F32),
            vm((2, 3, 4, 5, *tile), F32),
            vm((2, 3, 4, 2, 2, *tile), F32),
            vm((2, 2, 10, *tile), F32),
            vm((2, 4, 5, *tile), F32),
            vm((2, 4, 2, 2, *tile), F32),
            vm((2, 3, 5, *tile), F32),
            vm((2, 3, 5, *tile), F32),
            vm((2, 3, 2, 2, *tile), F32),
            vm((2, 2, 5, *tile), F32),
            vm((2, 2, 2, *tile), F32),
            vm((2, 3, 2, 5, *tile), F32),
            vm((2, 3, *tile), F32),
            vm((2, 2, 5, *tile), F32),
            vm((2, *tile), F32),
            vm((2, 2, 5, *tile), F32),
            vm((2, 7, *tile), F32),
            vm((2, TAPS, *tile), F32),
            dma((4,)),
            dma((4,)),
            dma((3, 8)),
            dma((3, 8)),
            dma((2,)),
            dma((2,)),
            dma((2, 3, 3)),
            dma((2, 3, 3)),
            dma((2, 3, 3)),
            dma((2, 3, 3)),
            dma((2, 2, 3)),
            dma((2, 2, 3)),
            dma((2, 8)),
            dma((2, 8)),
        ],
        compiler_params=pltpu.CompilerParams(
            collective_id=0, has_side_effects=True, vmem_limit_bytes=62 * 2**20
        ),
    )(occupancy, features.reshape(split), cotangent.reshape(split), w_first, w_second)
    return out.reshape(features.shape), grad.reshape(features.shape), first, second


def solution(mesh):
    in_specs = (P("gx", "gy", None, None), P(), P(), P("gx", "gy", None), P("gx", "gy", None, None))
    out_specs = (
        P("gx", "gy", None, None),
        P("gx", "gy", None, None),
        P(None, "gy", None),
        P(None, "gy", None),
    )
    return jax.shard_map(body, mesh=mesh, in_specs=in_specs, out_specs=out_specs, check_vma=False)
```

profile of v0, /device:TPU:0, one launch (start us, length us, event | category | flops | bytes accessed | tf_op | source)
XLA Modules:
  0.0 59.1 jit_solution(11819877204323559747)
XLA Ops:
  0.6 54.0 %section.1 = (bf16[8,8,2,16,128]{4,3,2,1,0:T(8,128)(2,1)}, bf16[8,8,2,16,128]{4,3,2,1,0:T(8,128)(2,1)}, f32[27,8,128]{2,1,0:T(8,128)}, f32[27,8,128]{2,1,0:T(8,128)}) custom-call(s32[1,2,2]{2,1,0:T(2,128)} %occ_ref.1, bf16[8,8,2,16,128]{4,3,2,1,0:T(8,128)(2,1)} %bitcast.4, bf16[8,8,2,16,128]{4,3,2,1,0:T(8,128)(2,1)} %bitcast.5, ...), custom_call_target="tpu_custom_call" | custom-call | tf_op jit(solution)/shard_map/section/pallas_call | solution.py:462
  54.6 0.0 copy-start
  54.6 1.9 %copy.13 = bf16[8,16,16,128]{3,2,1,0:T(8,128)(2,1)} copy(bf16[8,16,16,128]{3,2,1,0:T(8,128)(2,1)} %bitcast.7) | data formatting | bytes 1048576
  56.5 0.0 copy-done
  56.5 0.0 copy-start.2
  56.5 0.8 %copy.14 = bf16[8,16,16,128]{3,2,1,0:T(8,128)(2,1)} copy(bf16[8,16,16,128]{3,2,1,0:T(8,128)(2,1)S(1)} %bitcast.6) | data formatting | bytes 1048576
  57.3 0.2 copy-done.2
  57.5 0.0 copy-start.1
  57.5 0.6 %copy.15 = f32[27,8,128]{2,1,0:T(8,128)} copy(f32[27,8,128]{2,1,0:T(8,128)S(1)} %copy-done.2) | data formatting | bytes 221184
  58.2 0.3 copy-done.1
  58.5 0.6 %copy.16 = f32[27,8,128]{2,1,0:T(8,128)} copy(f32[27,8,128]{2,1,0:T(8,128)S(1)} %copy-done.1) | data formatting | bytes 221184
Async XLA Ops:
  54.6 1.9 %copy-start = (bf16[8,8,2,16,128]{4,3,2,1,0:T(8,128)(2,1)S(1)}, bf16[8,8,2,16,128]{4,3,2,1,0:T(8,128)(2,1)}, u32[]{:S(2)}) copy-start(bf16[8,8,2,16,128]{4,3,2,1,0:T(8,128)(2,1)} %get-tuple-element.9) | copy-start | bytes 1572868
  56.5 1.0 %copy-start.2 = (f32[27,8,128]{2,1,0:T(8,128)S(1)}, f32[27,8,128]{2,1,0:T(8,128)}, u32[]{:S(2)}) copy-start(f32[27,8,128]{2,1,0:T(8,128)} %get-tuple-element.18) | copy-start | bytes 331780
  57.5 0.9 %copy-start.1 = (f32[27,8,128]{2,1,0:T(8,128)S(1)}, f32[27,8,128]{2,1,0:T(8,128)}, u32[]{:S(2)}) copy-start(f32[27,8,128]{2,1,0:T(8,128)} %get-tuple-element.19) | copy-start | bytes 331780
where the time goes:
time: 59.5 us; the launch traced here: 59.1 us
  Pallas kernels  54 us (91%)
  local copies, waits for them, and re-layouts  4.51 us (8%)
  between operations  0.65 us (1%)
    pallas_call x1, Pallas kernels, body(): pl.pallas_call(functools.partial(kernel, scale), name='section', out_shap...  54 us
    unnamed x10, local copies, waits for them, and re-layouts  4.51 us

commit v1 on v0

v1 whole, which is shorter than its diff:
```python
import functools
import math

import jax
import jax.numpy as jnp
from jax import lax
from jax.experimental import pallas as pl
from jax.experimental.pallas import tpu as pltpu
from jax.sharding import PartitionSpec as P

F32 = jnp.float32
BF16 = jnp.bfloat16
MESH = pl.DeviceIdType.MESH
DIRS = [(ax, ay) for ax in (-1, 0, 1) for ay in (-1, 0, 1) if (ax, ay) != (0, 0)]
GX, GY = 8, 16
X, Y, Z, C = 8, 16, 16, 128
TAPS = 28
FRONT = [(0, 2, 0, 8)], [(2, 2, 0, 8)]
BACK = [(4, 2, 0, 8)], [(6, 2, 0, 8)]
INNER = [(1, 3, 1, 6)], [(4, 3, 1, 6)]
RIM = [(0, 1, 0, 8), (1, 6, 0, 1)], [(7, 1, 0, 8), (1, 6, 7, 1)]

FULL = ("x", "yh", "z", "yl")
SIZE = {"x": 4, "yh": 2, "z": 4, "yl": 2}
PARTS = (
    (0, FULL, ("x", "z", "y")),
    (8, FULL, ("y", "x", "z")),
    (16, FULL, ("z", "y", "x")),
    (24, FULL[:3], ("x", "y", "z")),
)


def without(dims, axis):
    gone = ("yh", "yl") if axis == "y" else (axis,)
    return tuple(d for d in dims if d not in gone)


def dims_after(part, stages):
    dims = part[1]
    for axis in part[2][:stages]:
        dims = without(dims, axis)
    return dims


def shape_of(dims):
    return tuple(SIZE[d] for d in dims) + (8, C)


def kernel(scale, names, *refs):
    ref = dict(zip(names, refs))
    occ_ref, feat_hbm, cot_hbm, w1_hbm, w2_hbm = (ref[n] for n in ("occ", "f_in", "c_in", "w1_in", "w2_in"))
    out_hbm, gf_hbm, g1_hbm, g2_hbm = (ref[n] for n in ("out", "gf", "g1", "g2"))
    feat, cot, w1, w2, fu, hq = (ref[n] for n in ("feat", "cot", "w1", "w2", "fu", "hq"))
    slope, at, outs, part, r0, fin, rfin, done = (
        ref[n] for n in ("slope", "at", "outs", "part", "r0", "fin", "rfin", "done")
    )
    in_sem, out_sem, hs, hr, s0s, s0r, rss, rsr, s4s, s4r = (
        ref[n] for n in ("in_sem", "out_sem", "hs", "hr", "s0s", "s0r", "rss", "rsr", "s4s", "s4r")
    )
    gx = lax.axis_index("gx")
    gy = lax.axis_index("gy")
    core = gy % 2
    px = (gy // 2) % 4
    yh = gy // 8
    pz = gx % 4
    yl = gx // 4
    py = yh * 2 + yl

    def at_x(k):
        return (px + k) % 4

    def at_y(k):
        return (py + k) % 4

    def at_z(k):
        return (pz + k) % 4

    def dev_x(k):
        return (gx, yh * 8 + at_x(k) * 2 + core)

    def dev_y(k):
        to = at_y(k)
        return ((to % 2) * 4 + pz, (to // 2) * 8 + px * 2 + core)

    def dev_z(k):
        return (yl * 4 + at_z(k), gy)

    partner = (gx, gy + 1 - 2 * core)

    def exists(ax, ay):
        ok = None
        for step, pos, size in ((ax, gx, GX), (ay, gy, GY)):
            if step == 0:
                continue
            here = pos + 1 < size if step > 0 else pos > 0
            ok = here if ok is None else jnp.logical_and(ok, here)
        return ok

    barrier = pltpu.get_barrier_semaphore()
    for ax, ay in DIRS:
        @pl.when(exists(ax, ay))
        def _():
            pl.semaphore_signal(barrier, inc=1, device_id=(gx + ax, gy + ay), device_id_type=MESH)
    fixed = [partner] + [dev_x(k) for k in (1, 2, 3)] + [dev_y(k) for k in (1, 2, 3)]
    fixed += [((gx + k) % GX, gy) for k in range(1, GX)]
    for peer in fixed:
        pl.semaphore_signal(barrier, inc=1, device_id=peer, device_id_type=MESH)

    loads = [
        pltpu.make_async_copy(src, dst, in_sem.at[i])
        for i, (src, dst) in enumerate(
            ((feat_hbm, feat), (cot_hbm, cot), (w1_hbm, w1), (w2_hbm, w2))
        )
    ]
    for load in loads:
        load.start()

    low = lax.broadcasted_iota(jnp.int32, (Z, C), 0) < 8
    mask = [
        jnp.where(low, occ_ref[0, b, 0].astype(F32), occ_ref[0, b, 1].astype(F32)) for b in range(2)
    ]

    def mask_rows(boxes, wide):
        rows = []
        for x0, nx, k0, nk in boxes:
            for _ in range(nx):
                rows += [mask[k // 4] for k in range(k0, k0 + nk)]
        m = jnp.concatenate(rows, axis=0)
        return jnp.concatenate([m, m], axis=1) if wide else m

    def z_shift(field, at_index):
        v = field[(1, *at_index)].astype(F32)
        t = v.reshape(-1, Z, C)
        z = lax.broadcasted_iota(jnp.int32, (1, Z, C), 1)
        down = jnp.where(z == 0, 0.0, pltpu.roll(t, 1, 1))
        up = jnp.where(z == Z - 1, 0.0, pltpu.roll(t, Z - 1, 1))
        field[(0, *at_index)] = down.astype(BF16).reshape(v.shape)
        field[(2, *at_index)] = up.astype(BF16).reshape(v.shape)

    def edge_x(step, recv):
        if step == 0:
            return (pl.ds(1, X),)
        if recv:
            return (0 if step > 0 else X + 1,)
        return (X if step > 0 else 1,)

    def edge_y(step, recv):
        if step == 0:
            return (pl.ds(1, 8),)
        if recv:
            return (0, 1) if step > 0 else (9, 0)
        return (8, 1) if step > 0 else (1, 0)

    def halo_copy(ref, d, slot):
        ax, ay = DIRS[d]
        return pltpu.make_async_remote_copy(
            src_ref=ref.at[(1, *edge_x(ax, False), *edge_y(ay, False))],
            dst_ref=ref.at[(1, *edge_x(ax, True), *edge_y(ay, True))],
            send_sem=hs.at[slot, d],
            recv_sem=hr.at[slot, d],
            device_id=(gx + ax, gy + ay),
            device_id_type=MESH,
        )

    def halo_start(ref, slot):
        for d, (ax, ay) in enumerate(DIRS):
            @pl.when(exists(ax, ay))
            def _():
                halo_copy(ref, d, slot).start()

    def halo_zero(ref):
        for ax, ay in DIRS:
            @pl.when(jnp.logical_not(exists(-ax, -ay)))
            def _():
                index = (1, *edge_x(ax, True), *edge_y(ay, True))
                ref[index] = jnp.zeros(ref.at[index].shape, BF16)

    def halo_wait(ref, slot):
        for d, (ax, ay) in enumerate(DIRS):
            @pl.when(exists(-ax, -ay))
            def _():
                halo_copy(ref, d, slot).wait_recv()

    def halo_sent(ref, slot):
        for d, (ax, ay) in enumerate(DIRS):
            @pl.when(exists(ax, ay))
            def _():
                halo_copy(ref, d, slot).wait_send()

    def shift_rim(field):
        for x in (0, X + 1):
            z_shift(field, (x,))
        for edge in ((0, 1), (9, 0)):
            z_shift(field, (pl.ds(1, X), *edge))

    def shift_inner(field):
        for x in range(1, X + 1):
            z_shift(field, (x, pl.ds(1, 8)))

    def rows_of(field, boxes, dz, dx, j):
        halves = []
        for h in range(2):
            pieces = [
                field[dz, pl.ds(x0 + dx, nx), pl.ds(k0 + j + h, nk), 1 - h].reshape(nx * nk * Z, C)
                for x0, nx, k0, nk in boxes
            ]
            halves.append(jnp.concatenate(pieces, axis=0) if len(pieces) > 1 else pieces[0])
        return jnp.concatenate(halves, axis=1)

    zero = jnp.zeros((C, C), BF16)

    def conv(field, w, boxes, flipped):
        left, right = [], []
        for dx in range(3):
            for dz in range(3):
                tap = [w[26 - (9 * dx + 3 * dy + dz)] if flipped else w[9 * dx + 3 * dy + dz] for dy in range(3)]
                for j in range(2):
                    left.append(rows_of(field, boxes, dz, dx, j))
                    if j == 0:
                        grid = ((tap[0], zero), (tap[1], tap[0]))
                    else:
                        grid = ((tap[2], tap[1]), (zero, tap[2]))
                    if flipped:
                        grid = tuple(zip(*grid))
                        right.append(jnp.concatenate([jnp.concatenate(r, axis=1) for r in grid], axis=0))
                    else:
                        right.append(jnp.concatenate([jnp.concatenate(r, axis=1) for r in grid], axis=0))
        lhs = jnp.concatenate(left, axis=1)
        if flipped:
            return lax.dot_general(
                lhs, jnp.concatenate(right, axis=1), (((1,), (1,)), ((), ())), preferred_element_type=F32
            )
        return jnp.dot(lhs, jnp.concatenate(right, axis=0), preferred_element_type=F32)

    def tiles(boxes):
        at_row = 0
        for x0, nx, k0, nk in boxes:
            n = nx * nk * Z
            yield (x0, nx, k0, nk), slice(at_row, at_row + n)
            at_row += n

    def put(field_at, boxes, value):
        for (x0, nx, k0, nk), rows in tiles(boxes):
            for h in range(2):
                field_at(x0, nx, k0, nk, h, value[rows, h * C : (h + 1) * C].reshape(nx, nk, Z, C))

    def put_padded(field):
        def store(x0, nx, k0, nk, h, v):
            field[1, pl.ds(x0 + 1, nx), pl.ds(k0 + 1, nk), h] = v.astype(BF16)
        return store

    def forward(pair):
        pres = [conv(fu.at[0], w1, boxes, False) for boxes in pair]
        for pre, boxes in zip(pres, pair):
            s = jax.nn.sigmoid(pre)
            m = mask_rows(boxes, True)
            put(put_padded(hq.at[0]), boxes, m * (pre * s))
            d = m * (s * (1.0 + pre * (1.0 - s)))
            for (x0, nx, k0, nk), rows in tiles(boxes):
                slope[pl.ds(x0, nx), pl.ds(k0, nk)] = d[rows].reshape(nx, nk, Z, 2 * C)

    def backward(pair):
        grads = [conv(fu.at[1], w2, boxes, True) for boxes in pair]
        for grad, boxes in zip(grads, pair):
            d = [slope[pl.ds(x0, nx), pl.ds(k0, nk)].reshape(nx * nk * Z, 2 * C) for x0, nx, k0, nk in boxes]
            d = jnp.concatenate(d, axis=0) if len(d) > 1 else d[0]
            put(put_padded(hq.at[1]), boxes, grad * d)

    def finish(slot, w, flipped, pair):
        accs = [conv(hq.at[slot], w, boxes, flipped) for boxes in pair]
        base = fu.at[slot]

        def store(x0, nx, k0, nk, h, v):
            b = base[1, pl.ds(x0 + 1, nx), pl.ds(k0 + 1, nk), h].astype(F32)
            outs[slot, pl.ds(x0, nx), pl.ds(k0, nk), h] = (b + v).astype(BF16)
        for acc, boxes in zip(accs, pair):
            put(store, boxes, acc * mask_rows(boxes, True))

    def turn(left):
        for h in range(2):
            for x in range(X):
                at[h, x] = left[1, x + 1, pl.ds(1, 8), h].reshape(8 * Z, C).T

    def wgrad(g, p, right, mirrored):
        lhs = jnp.concatenate([at[h, x] for h in range(2) for x in range(X)], axis=1)
        first = PARTS[p][0]
        middle = first + 4 if p < 3 else first + 2
        pair = range(first, middle), range(middle, min(first + 8, 27))
        sums = []
        for taps in pair:
            cols = []
            for tap in taps:
                dx, dy, dz = tap // 9, tap // 3 % 3, tap % 3
                ex, ey, ez = (2 - dx, 2 - dy, 2 - dz) if mirrored else (dx, dy, dz)
                halves = []
                for h in range(2):
                    row = h + ey + 1
                    halves.append(right[ez, pl.ds(ex, X), pl.ds(row // 2, 8), row % 2].reshape(X * 8 * Z, C))
                cols.append(jnp.concatenate(halves, axis=0))
            rhs = jnp.concatenate(cols, axis=1) if len(cols) > 1 else cols[0]
            sums.append(jnp.dot(lhs, rhs, preferred_element_type=F32))
        for acc, taps in zip(sums, pair):
            for i, tap in enumerate(taps):
                block = acc[:, i * C : (i + 1) * C]
                if not mirrored:
                    block = block.T
                for s in range(16):
                    part[g, s % 2, (s // 2) % 4, s // 8, tap] = block[8 * s : 8 * s + 8]
        start(stage0(g, p))

    def remote(src, dst, send, recv, to):
        return pltpu.make_async_remote_copy(
            src_ref=src, dst_ref=dst, send_sem=send, recv_sem=recv, device_id=to, device_id_type=MESH
        )

    def count(p):
        return 8 if p < 3 else 4

    def stage0(g, p):
        taps = pl.ds(PARTS[p][0], count(p))
        return [
            remote(
                part.at[g, 1 - core, :, :, taps], r0.at[g, :, :, taps], s0s.at[g, p], s0r.at[g, p], partner
            )
        ]

    def pick(dims, axis, pos):
        index = []
        for d in dims:
            if d == axis:
                index.append(pos)
            elif axis == "y" and d == "yh":
                index.append(pos // 2)
            elif axis == "y" and d == "yl":
                index.append(pos % 2)
            else:
                index.append(slice(None))
        return tuple(index)

    position = {"x": (at_x, dev_x), "y": (at_y, dev_y), "z": (at_z, dev_z)}

    def ring(g, p, stage):
        dims = dims_after(PARTS[p], stage - 1)
        axis = PARTS[p][2][stage - 1]
        where, device = position[axis]
        source = ref[f"h{p}"] if stage == 1 else ref[f"t{p}_{stage - 1}"]
        return [
            remote(
                source.at[(g, *pick(dims, axis, where(k)))],
                ref[f"r{p}_{stage}"].at[g, k - 1],
                rss.at[g, p, stage - 1, k - 1],
                rsr.at[g, p, stage - 1, k - 1],
                device(k),
            )
            for k in (1, 2, 3)
        ]

    def gather(g):
        return [
            remote(fin.at[g], rfin.at[g, k - 1], s4s.at[g, k - 1], s4r.at[g, k - 1], ((gx + k) % GX, gy))
            for k in range(1, GX)
        ]

    def start(copies):
        for copy in copies:
            copy.start()

    def arrive(copies):
        for copy in copies:
            copy.wait_recv()

    def step0(g, p):
        arrive(stage0(g, p))
        first = PARTS[p][0]
        for i in range(count(p)):
            total = part[g, core, :, :, first + i] + r0[g, :, :, first + i]
            index = (g, slice(None), slice(None)) + ((i // 2, i % 2) if p < 3 else (i,))
            ref[f"t{p}_0"][index] = total
            ref[f"h{p}"][index] = total.astype(BF16)
        start(ring(g, p, 1))

    def step(g, p, stage):
        arrive(ring(g, p, stage))
        dims = dims_after(PARTS[p], stage - 1)
        axis = PARTS[p][2][stage - 1]
        own = ref[f"t{p}_{stage - 1}"][(g, *pick(dims, axis, position[axis][0](0)))]
        r = ref[f"r{p}_{stage}"]
        total = (own + r[g, 0].astype(F32)) + (r[g, 1].astype(F32) + r[g, 2].astype(F32))
        if stage < 3:
            ref[f"t{p}_{stage}"][g] = total
            start(ring(g, p, stage + 1))
        else:
            fin[g, p] = total

    def spread(g):
        start(gather(g))

    def collect(g, target, sem):
        for p in range(3):
            done[g, 8 * p + 2 * pz + yl] = fin[g, p] * scale

        @pl.when(yl == 0)
        def _():
            done[g, 24 + pz] = fin[g, 3] * scale
        for k, copy in enumerate(gather(g), 1):
            copy.wait_recv()
            source = (gx + GX - k) % GX
            for p in range(3):
                done[g, 8 * p + 2 * (source % 4) + source // 4] = rfin[g, k - 1, p] * scale

            @pl.when(source < 4)
            def _():
                done[g, 24 + source] = rfin[g, k - 1, 3] * scale
        copy = pltpu.make_async_copy(done.at[g, pl.ds(0, 27)], target, out_sem.at[sem])
        copy.start()
        return copy

    for g in range(2):
        part[g, :, :, :, 27] = jnp.zeros((2, 4, 2, 8, C), F32)

    for f, raw in enumerate((feat, cot)):
        loads[f].wait()
        for x in range(X):
            for b in range(2):
                rows = raw[x, pl.ds(4 * b, 4)].astype(F32) * mask[b][None, None]
                fu[f, 1, x + 1, pl.ds(4 * b + 1, 4)] = rows.astype(BF16)
    for f in range(2):
        halo_zero(fu.at[f])
        halo_zero(hq.at[f])

    wide_x = 1 + (gx > 0).astype(jnp.int32) + (gx < GX - 1).astype(jnp.int32)
    wide_y = 1 + (gy > 0).astype(jnp.int32) + (gy < GY - 1).astype(jnp.int32)
    pl.semaphore_wait(barrier, len(fixed) + wide_x * wide_y - 1)

    halo_start(fu.at[0], 0)
    halo_start(fu.at[1], 1)
    for f in range(2):
        shift_inner(fu.at[f])
    loads[2].wait()
    loads[3].wait()
    forward(INNER)
    backward(INNER)
    halo_wait(fu.at[0], 0)
    shift_rim(fu.at[0])
    forward(RIM)
    halo_start(hq.at[0], 2)
    halo_wait(fu.at[1], 1)
    shift_rim(fu.at[1])
    turn(hq.at[0])
    wgrad(1, 0, fu.at[1], True)
    wgrad(1, 1, fu.at[1], True)
    wgrad(1, 2, fu.at[1], True)
    step0(1, 0)
    wgrad(1, 3, fu.at[1], True)
    step0(1, 1)
    backward(RIM)
    halo_start(hq.at[1], 3)
    step0(1, 2)
    step0(1, 3)
    turn(hq.at[1])
    wgrad(0, 0, fu.at[0], False)
    wgrad(0, 1, fu.at[0], False)
    wgrad(0, 2, fu.at[0], False)
    step0(0, 0)
    wgrad(0, 3, fu.at[0], False)
    step0(0, 1)
    shift_inner(hq.at[0])
    halo_wait(hq.at[0], 2)
    shift_rim(hq.at[0])
    step0(0, 2)
    step(1, 0, 1)
    step(1, 1, 1)
    step0(0, 3)
    step(1, 2, 1)
    step(1, 3, 1)
    finish(0, w2, False, FRONT)
    step(1, 0, 2)
    step(1, 1, 2)
    step(1, 2, 2)
    step(1, 3, 2)
    finish(0, w2, False, BACK)
    out_copy = pltpu.make_async_copy(outs.at[0], out_hbm, out_sem.at[0])
    out_copy.start()
    step(0, 0, 1)
    step(0, 1, 1)
    shift_inner(hq.at[1])
    halo_wait(hq.at[1], 3)
    shift_rim(hq.at[1])
    step(0, 2, 1)
    step(0, 3, 1)
    finish(1, w1, True, FRONT)
    step(1, 0, 3)
    step(1, 1, 3)
    step(1, 2, 3)
    step(1, 3, 3)
    spread(1)
    step(0, 0, 2)
    step(0, 1, 2)
    step(0, 2, 2)
    step(0, 3, 2)
    finish(1, w1, True, BACK)
    gf_copy = pltpu.make_async_copy(outs.at[1], gf_hbm, out_sem.at[1])
    gf_copy.start()
    step(0, 0, 3)
    step(0, 1, 3)
    step(0, 2, 3)
    step(0, 3, 3)
    spread(0)
    g2_copy = collect(1, g2_hbm, 2)
    g1_copy = collect(0, g1_hbm, 3)

    for slot, field in enumerate((fu.at[0], fu.at[1], hq.at[0], hq.at[1])):
        halo_sent(field, slot)
    for g in range(2):
        sent = gather(g)
        for p in range(4):
            sent += stage0(g, p) + ring(g, p, 1) + ring(g, p, 2) + ring(g, p, 3)
        for copy in sent:
            copy.wait_send()
    for copy in (out_copy, gf_copy, g2_copy, g1_copy):
        copy.wait()


def hand_on(a, b, c, d, a_out, b_out, c_out, d_out):
    for source, target in ((a, a_out), (b, b_out), (c, c_out), (d, d_out)):
        target[...] = source[...]


def body(features, w_first, w_second, occupancy, cotangent):
    scale = 1.0 / math.sqrt(GX * GY * X * Y * Z)
    anyspace = pl.BlockSpec(memory_space=pl.ANY)
    dma = pltpu.SemaphoreType.DMA
    vm = pltpu.VMEM
    split = (X, 8, 2, Z, C)
    field = (2, 3, X + 2, 10, 2, Z, C)
    tile = (8, C)
    scratch = {
        "feat": vm(split, BF16),
        "cot": vm(split, BF16),
        "w1": vm((27, C, C), BF16),
        "w2": vm((27, C, C), BF16),
        "fu": vm(field, BF16),
        "hq": vm(field, BF16),
        "slope": vm((X, 8, Z, 2 * C), F32),
        "at": vm((2, X, C, 8 * Z), BF16),
        "outs": vm((2, *split), BF16),
        "part": vm((2, 2, 4, 2, TAPS, *tile), F32),
        "r0": vm((2, 4, 2, TAPS, *tile), F32),
        "fin": vm((2, 4, *tile), F32),
        "rfin": vm((2, 7, 4, *tile), F32),
        "done": vm((2, TAPS, *tile), F32),
        "in_sem": dma((4,)),
        "out_sem": dma((4,)),
        "hs": dma((4, 8)),
        "hr": dma((4, 8)),
        "s0s": dma((2, 4)),
        "s0r": dma((2, 4)),
        "rss": dma((2, 4, 3, 3)),
        "rsr": dma((2, 4, 3, 3)),
        "s4s": dma((2, 7)),
        "s4r": dma((2, 7)),
    }
    for p, part in enumerate(PARTS):
        scratch[f"h{p}"] = vm((2, *shape_of(part[1])), BF16)
        for stage in range(4):
            shape = shape_of(dims_after(part, stage))
            if stage < 3:
                scratch[f"t{p}_{stage}"] = vm((2, *shape), F32)
            if stage > 0:
                scratch[f"r{p}_{stage}"] = vm((2, 3, *shape), BF16 if stage == 1 else F32)
    names = ("occ", "f_in", "c_in", "w1_in", "w2_in", "out", "gf", "g1", "g2", *scratch)
    shapes = (
        jax.ShapeDtypeStruct(split, BF16),
        jax.ShapeDtypeStruct(split, BF16),
        jax.ShapeDtypeStruct((27, 8, C), F32),
        jax.ShapeDtypeStruct((27, 8, C), F32),
    )
    stay = [
        pltpu.with_memory_space_constraint(a, pltpu.HBM)
        for a in (features.reshape(split), cotangent.reshape(split), w_first, w_second)
    ]
    results = pl.pallas_call(
        functools.partial(kernel, scale, names),
        name="section",
        out_shape=shapes,
        in_specs=[pl.BlockSpec(memory_space=pltpu.SMEM)] + [pl.BlockSpec(memory_space=pltpu.HBM)] * 4,
        out_specs=(anyspace,) * 4,
        scratch_shapes=list(scratch.values()),
        compiler_params=pltpu.CompilerParams(
            collective_id=0, has_side_effects=True, vmem_limit_bytes=48 * 2**20
        ),
    )(occupancy, *stay)
    local = pl.BlockSpec(memory_space=pltpu.VMEM)
    out, grad, first, second = pl.pallas_call(
        hand_on,
        name="hand_on",
        out_shape=shapes,
        in_specs=[local] * 4,
        out_specs=(local,) * 4,
        compiler_params=pltpu.CompilerParams(vmem_limit_bytes=8 * 2**20),
    )(*results)
    return out.reshape(features.shape), grad.reshape(features.shape), first, second


def solution(mesh):
    in_specs = (P("gx", "gy", None, None), P(), P(), P("gx", "gy", None), P("gx", "gy", None, None))
    out_specs = (
        P("gx", "gy", None, None),
        P("gx", "gy", None, None),
        P(None, "gy", None),
        P(None, "gy", None),
    )
    return jax.shard_map(body, mesh=mesh, in_specs=in_specs, out_specs=out_specs, check_vma=False)
```

time: 59.5 us -> 46.8 us (0.79)
  Pallas kernels: 54 us -> 45.4 us
  local copies, waits for them, and re-layouts: 4.51 us -> 0.67 us
    pallas_call x1 -> x2, Pallas kernels: 54 us -> 45.4 us  [the longest x1 44.2 us: body(): pl.pallas_call(functools.partial(kernel, scale, names), name='section', o...]
    unnamed x10 -> x2, local copies, waits for them, and re-layouts: 4.51 us -> 0.67 us
where the time goes in v1:
time: 46.8 us; the launch traced here: 46.7 us
  Pallas kernels  45.4 us (97%)
  local copies, waits for them, and re-layouts  0.67 us (1%)
  between operations  0.65 us (1%)
    pallas_call x1, Pallas kernels, body(): pl.pallas_call(functools.partial(kernel, scale, names), name='section', o...  44.2 us
    pallas_call x1, Pallas kernels, body(): pl.pallas_call(hand_on, name='hand_on', out_shape=shapes, in_specs=[local...  1.11 us

profile of v1, /device:TPU:0, one launch (start us, length us, event | category | flops | bytes accessed | tf_op | source)
XLA Modules:
  0.0 46.7 jit_solution(11242328272872652162)
XLA Ops:
  0.6 0.0 copy-start
  0.6 0.7 %copy-done = s32[1,2,2]{2,1,0:T(2,128)S(1)} copy-done((s32[1,2,2]{2,1,0:T(2,128)S(1)}, s32[1,2,2]{2,1,0:T(2,128)}, u32[]{:S(2)}) %copy-start) | copy-done | bytes 40
  1.3 44.2 %section.1 = (bf16[8,8,2,16,128]{4,3,2,1,0:T(8,128)(2,1)S(1)}, bf16[8,8,2,16,128]{4,3,2,1,0:T(8,128)(2,1)S(1)}, f32[27,8,128]{2,1,0:T(8,128)S(1)}, f32[27,8,128]{2,1,0:T(8,128)S(1)}) custom-call(s32[1,2,2]{2,1,0:T(2,128)S(1)} %copy-done, bf16[8,8,2,16,128]{4,3,2,1,0:T(8,128)(2,1)} %bitcast.4, bf16[8,8,2,16,128]{4,3,2,1,0:T(8,128)(2,1)} %bitcast.5, ...), custom_call_target="tpu_custom_call" | custom-call | tf_op jit(solution)/shard_map/section/pallas_call | solution.py:582
  45.6 1.1 %hand_on.1 = (bf16[8,8,2,16,128]{4,3,2,1,0:T(8,128)(2,1)}, bf16[8,8,2,16,128]{4,3,2,1,0:T(8,128)(2,1)}, f32[27,8,128]{2,1,0:T(8,128)}, f32[27,8,128]{2,1,0:T(8,128)}) custom-call(bf16[8,8,2,16,128]{4,3,2,1,0:T(8,128)(2,1)S(1)} %get-tuple-element.12.a, bf16[8,8,2,16,128]{4,3,2,1,0:T(8,128)(2,1)S(1)} %get-tuple-element.13.b, ...), custom_call_target="tpu_custom_call" | custom-call | tf_op jit(solution)/shard_map/hand_on/pallas_call | solution.py:594
Async XLA Ops:
  0.6 0.7 %copy-start = (s32[1,2,2]{2,1,0:T(2,128)S(1)}, s32[1,2,2]{2,1,0:T(2,128)}, u32[]{:S(2)}) copy-start(s32[1,2,2]{2,1,0:T(2,128)} %refs_0_.1) | copy-start | bytes 52

commit v2 on v1

--- a/solution.py
+++ b/solution.py
@@ -48,12 +48,13 @@
 
 def kernel(scale, names, *refs):
     ref = dict(zip(names, refs))
-    occ_ref, feat_hbm, cot_hbm, w1_hbm, w2_hbm = (ref[n] for n in ("occ", "f_in", "c_in", "w1_in", "w2_in"))
+    occ_hbm, feat_hbm, cot_hbm, w1_hbm, w2_hbm = (ref[n] for n in ("occ", "f_in", "c_in", "w1_in", "w2_in"))
     out_hbm, gf_hbm, g1_hbm, g2_hbm = (ref[n] for n in ("out", "gf", "g1", "g2"))
     feat, cot, w1, w2, fu, hq = (ref[n] for n in ("feat", "cot", "w1", "w2", "fu", "hq"))
     slope, at, outs, part, r0, fin, rfin, done = (
         ref[n] for n in ("slope", "at", "outs", "part", "r0", "fin", "rfin", "done")
     )
+    occ_ref, occ_sem = ref["occ_here"], ref["occ_sem"]
     in_sem, out_sem, hs, hr, s0s, s0r, rss, rsr, s4s, s4r = (
         ref[n] for n in ("in_sem", "out_sem", "hs", "hr", "s0s", "s0r", "rss", "rsr", "s4s", "s4r")
     )
@@ -96,6 +97,21 @@
             ok = here if ok is None else jnp.logical_and(ok, here)
         return ok
 
+    get_occ = pltpu.make_async_copy(occ_hbm, occ_ref, occ_sem.at[0])
+    get_occ.start()
+    loads = [
+        [
+            pltpu.make_async_copy(src.at[pl.ds(2 * i, 2)], dst.at[pl.ds(2 * i, 2)], in_sem.at[f, i])
+            for i in range(4)
+        ]
+        for f, (src, dst) in enumerate(((feat_hbm, feat), (cot_hbm, cot)))
+    ]
+    loads += [
+        [pltpu.make_async_copy(src, dst, in_sem.at[f, 0])] for f, src, dst in ((2, w1_hbm, w1), (3, w2_hbm, w2))
+    ]
+    for group in loads:
+        for load in group:
+            load.start()
     barrier = pltpu.get_barrier_semaphore()
     for ax, ay in DIRS:
         @pl.when(exists(ax, ay))
@@ -106,15 +122,7 @@
     for peer in fixed:
         pl.semaphore_signal(barrier, inc=1, device_id=peer, device_id_type=MESH)
 
-    loads = [
-        pltpu.make_async_copy(src, dst, in_sem.at[i])
-        for i, (src, dst) in enumerate(
-            ((feat_hbm, feat), (cot_hbm, cot), (w1_hbm, w1), (w2_hbm, w2))
-        )
-    ]
-    for load in loads:
-        load.start()
-
+    get_occ.wait()
     low = lax.broadcasted_iota(jnp.int32, (Z, C), 0) < 8
     mask = [
         jnp.where(low, occ_ref[0, b, 0].astype(F32), occ_ref[0, b, 1].astype(F32)) for b in range(2)
@@ -348,18 +356,25 @@
             remote(
                 source.at[(g, *pick(dims, axis, where(k)))],
                 ref[f"r{p}_{stage}"].at[g, k - 1],
-                rss.at[g, p, stage - 1, k - 1],
-                rsr.at[g, p, stage - 1, k - 1],
+                rss.at[g, p, stage - 1],
+                rsr.at[g, p, stage - 1],
                 device(k),
             )
             for k in (1, 2, 3)
         ]
 
+    def three(g, p, stage):
+        every = ref[f"r{p}_{stage}"].at[g]
+        return remote(every, every, rss.at[g, p, stage - 1], rsr.at[g, p, stage - 1], partner)
+
     def gather(g):
         return [
-            remote(fin.at[g], rfin.at[g, k - 1], s4s.at[g, k - 1], s4r.at[g, k - 1], ((gx + k) % GX, gy))
+            remote(fin.at[g], rfin.at[g, k - 1], s4s.at[g], s4r.at[g], ((gx + k) % GX, gy))
             for k in range(1, GX)
         ]
+
+    def seven(g):
+        return remote(rfin.at[g], rfin.at[g], s4s.at[g], s4r.at[g], partner)
 
     def start(copies):
         for copy in copies:
@@ -380,7 +395,7 @@
         start(ring(g, p, 1))
 
     def step(g, p, stage):
-        arrive(ring(g, p, stage))
+        three(g, p, stage).wait_recv()
         dims = dims_after(PARTS[p], stage - 1)
         axis = PARTS[p][2][stage - 1]
         own = ref[f"t{p}_{stage - 1}"][(g, *pick(dims, axis, position[axis][0](0)))]
@@ -392,6 +407,15 @@
         else:
             fin[g, p] = total
 
+    def settle(g):
+        for p in range(4):
+            stage0(g, p)[0].wait_send()
+            three(g, p, 1).wait_send()
+            three(g, p, 2).wait_send()
+            if g == 0:
+                three(1, p, 3).wait_send()
+                three(0, p, 3).wait_send()
+
     def spread(g):
         start(gather(g))
 
@@ -402,8 +426,8 @@
         @pl.when(yl == 0)
         def _():
             done[g, 24 + pz] = fin[g, 3] * scale
-        for k, copy in enumerate(gather(g), 1):
-            copy.wait_recv()
+        seven(g).wait_recv()
+        for k in range(1, GX):
             source = (gx + GX - k) % GX
             for p in range(3):
                 done[g, 8 * p + 2 * (source % 4) + source // 4] = rfin[g, k - 1, p] * scale
@@ -415,31 +439,30 @@
         copy.start()
         return copy
 
-    for g in range(2):
-        part[g, :, :, :, 27] = jnp.zeros((2, 4, 2, 8, C), F32)
-
     for f, raw in enumerate((feat, cot)):
-        loads[f].wait()
         for x in range(X):
+            if x % 2 == 0:
+                loads[f][x // 2].wait()
             for b in range(2):
                 rows = raw[x, pl.ds(4 * b, 4)].astype(F32) * mask[b][None, None]
                 fu[f, 1, x + 1, pl.ds(4 * b + 1, 4)] = rows.astype(BF16)
+    wide_x = 1 + (gx > 0).astype(jnp.int32) + (gx < GX - 1).astype(jnp.int32)
+    wide_y = 1 + (gy > 0).astype(jnp.int32) + (gy < GY - 1).astype(jnp.int32)
+    pl.semaphore_wait(barrier, len(fixed) + wide_x * wide_y - 1)
+
+    halo_start(fu.at[0], 0)
+    shift_inner(fu.at[0])
+    loads[2][0].wait()
+    forward(INNER)
+    halo_start(fu.at[1], 1)
+    shift_inner(fu.at[1])
+    loads[3][0].wait()
+    backward(INNER)
     for f in range(2):
         halo_zero(fu.at[f])
         halo_zero(hq.at[f])
-
-    wide_x = 1 + (gx > 0).astype(jnp.int32) + (gx < GX - 1).astype(jnp.int32)
-    wide_y = 1 + (gy > 0).astype(jnp.int32) + (gy < GY - 1).astype(jnp.int32)
-    pl.semaphore_wait(barrier, len(fixed) + wide_x * wide_y - 1)
-
-    halo_start(fu.at[0], 0)
-    halo_start(fu.at[1], 1)
-    for f in range(2):
-        shift_inner(fu.at[f])
-    loads[2].wait()
-    loads[3].wait()
-    forward(INNER)
-    backward(INNER)
+    for g in range(2):
+        part[g, :, :, :, 27] = jnp.zeros((2, 4, 2, 8, C), F32)
     halo_wait(fu.at[0], 0)
     shift_rim(fu.at[0])
     forward(RIM)
@@ -465,65 +488,72 @@
     wgrad(0, 3, fu.at[0], False)
     step0(0, 1)
     shift_inner(hq.at[0])
+    step0(0, 2)
+    step0(0, 3)
+    step(1, 0, 1)
+    step(1, 1, 1)
     halo_wait(hq.at[0], 2)
     shift_rim(hq.at[0])
-    step0(0, 2)
-    step(1, 0, 1)
-    step(1, 1, 1)
-    step0(0, 3)
+    finish(0, w2, False, FRONT)
     step(1, 2, 1)
     step(1, 3, 1)
-    finish(0, w2, False, FRONT)
+    finish(0, w2, False, BACK)
+    out_copy = pltpu.make_async_copy(outs.at[0], out_hbm, out_sem.at[0])
+    out_copy.start()
+    shift_inner(hq.at[1])
+    step(0, 0, 1)
+    step(0, 1, 1)
+    halo_wait(hq.at[1], 3)
+    shift_rim(hq.at[1])
+    finish(1, w1, True, FRONT)
+    step(0, 2, 1)
+    step(0, 3, 1)
     step(1, 0, 2)
     step(1, 1, 2)
     step(1, 2, 2)
     step(1, 3, 2)
-    finish(0, w2, False, BACK)
-    out_copy = pltpu.make_async_copy(outs.at[0], out_hbm, out_sem.at[0])
-    out_copy.start()
-    step(0, 0, 1)
-    step(0, 1, 1)
-    shift_inner(hq.at[1])
-    halo_wait(hq.at[1], 3)
-    shift_rim(hq.at[1])
-    step(0, 2, 1)
-    step(0, 3, 1)
-    finish(1, w1, True, FRONT)
+    finish(1, w1, True, BACK)
+    gf_copy = pltpu.make_async_copy(outs.at[1], gf_hbm, out_sem.at[1])
+    gf_copy.start()
+    step(0, 0, 2)
+    step(0, 1, 2)
+    step(0, 2, 2)
+    step(0, 3, 2)
     step(1, 0, 3)
     step(1, 1, 3)
     step(1, 2, 3)
     step(1, 3, 3)
     spread(1)
-    step(0, 0, 2)
-    step(0, 1, 2)
-    step(0, 2, 2)
-    step(0, 3, 2)
-    finish(1, w1, True, BACK)
-    gf_copy = pltpu.make_async_copy(outs.at[1], gf_hbm, out_sem.at[1])
-    gf_copy.start()
+    settle(1)
     step(0, 0, 3)
     step(0, 1, 3)
     step(0, 2, 3)
     step(0, 3, 3)
     spread(0)
     g2_copy = collect(1, g2_hbm, 2)
-    g1_copy = collect(0, g1_hbm, 3)
-
     for slot, field in enumerate((fu.at[0], fu.at[1], hq.at[0], hq.at[1])):
         halo_sent(field, slot)
+    settle(0)
+    out_copy.wait()
+    gf_copy.wait()
+    g1_copy = collect(0, g1_hbm, 3)
+
     for g in range(2):
-        sent = gather(g)
-        for p in range(4):
-            sent += stage0(g, p) + ring(g, p, 1) + ring(g, p, 2) + ring(g, p, 3)
-        for copy in sent:
-            copy.wait_send()
-    for copy in (out_copy, gf_copy, g2_copy, g1_copy):
+        seven(g).wait_send()
+    for copy in (g2_copy, g1_copy):
         copy.wait()
 
 
-def hand_on(a, b, c, d, a_out, b_out, c_out, d_out):
-    for source, target in ((a, a_out), (b, b_out), (c, c_out), (d, d_out)):
-        target[...] = source[...]
+def hand_on(*refs):
+    sources, targets, sems = refs[:4], refs[4:8], refs[8]
+    copies = [
+        pltpu.make_async_copy(source, target, sems.at[i])
+        for i, (source, target) in enumerate(zip(sources, targets))
+    ]
+    for copy in copies:
+        copy.start()
+    for copy in copies:
+        copy.wait()
 
 
 def body(features, w_first, w_second, occupancy, cotangent):
@@ -549,16 +579,18 @@
         "fin": vm((2, 4, *tile), F32),
         "rfin": vm((2, 7, 4, *tile), F32),
         "done": vm((2, TAPS, *tile), F32),
-        "in_sem": dma((4,)),
+        "occ_here": pltpu.SMEM((1, 2, 2), jnp.int32),
+        "occ_sem": dma((1,)),
+        "in_sem": dma((4, 4)),
         "out_sem": dma((4,)),
         "hs": dma((4, 8)),
         "hr": dma((4, 8)),
         "s0s": dma((2, 4)),
         "s0r": dma((2, 4)),
-        "rss": dma((2, 4, 3, 3)),
-        "rsr": dma((2, 4, 3, 3)),
-        "s4s": dma((2, 7)),
-        "s4r": dma((2, 7)),
+        "rss": dma((2, 4, 3)),
+        "rsr": dma((2, 4, 3)),
+        "s4s": dma((2,)),
+        "s4r": dma((2,)),
     }
     for p, part in enumerate(PARTS):
         scratch[f"h{p}"] = vm((2, *shape_of(part[1])), BF16)
@@ -577,26 +609,26 @@
     )
     stay = [
         pltpu.with_memory_space_constraint(a, pltpu.HBM)
-        for a in (features.reshape(split), cotangent.reshape(split), w_first, w_second)
+        for a in (occupancy, features.reshape(split), cotangent.reshape(split), w_first, w_second)
     ]
     results = pl.pallas_call(
         functools.partial(kernel, scale, names),
         name="section",
         out_shape=shapes,
-        in_specs=[pl.BlockSpec(memory_space=pltpu.SMEM)] + [pl.BlockSpec(memory_space=pltpu.HBM)] * 4,
+        in_specs=[pl.BlockSpec(memory_space=pltpu.HBM)] * 5,
         out_specs=(anyspace,) * 4,
         scratch_shapes=list(scratch.values()),
         compiler_params=pltpu.CompilerParams(
             collective_id=0, has_side_effects=True, vmem_limit_bytes=48 * 2**20
         ),
-    )(occupancy, *stay)
-    local = pl.BlockSpec(memory_space=pltpu.VMEM)
+    )(*stay)
     out, grad, first, second = pl.pallas_call(
         hand_on,
         name="hand_on",
         out_shape=shapes,
-        in_specs=[local] * 4,
-        out_specs=(local,) * 4,
+        in_specs=[anyspace] * 4,
+        out_specs=(anyspace,) * 4,
+        scratch_shapes=[dma((4,))],
         compiler_params=pltpu.CompilerParams(vmem_limit_bytes=8 * 2**20),
     )(*results)
     return out.reshape(features.shape), grad.reshape(features.shape), first, second

time: 46.8 us -> 42.7 us (0.912)
  Pallas kernels: 45.4 us -> 41.8 us
  local copies, waits for them, and re-layouts: 0.67 us -> 0 us
    pallas_call x1, Pallas kernels: 44.2 us -> 40.7 us  [body(): pl.pallas_call(functools.partial(kernel, scale, names), name='section', o...]
    unnamed x2 -> x0, local copies, waits for them, and re-layouts: 0.67 us -> none
where the time goes in v2:
time: 42.7 us; the launch traced here: 42.6 us
  Pallas kernels  41.8 us (98%)
  between operations  0.8 us (2%)
    pallas_call x1, Pallas kernels, body(): pl.pallas_call(functools.partial(kernel, scale, names), name='section', o...  40.7 us
    pallas_call x1, Pallas kernels, body(): pl.pallas_call(hand_on, name='hand_on', out_shape=shapes, in_specs=[anysp...  1.06 us

profile of v2, /device:TPU:0, one launch (start us, length us, event | category | flops | bytes accessed | tf_op | source)
XLA Modules:
  0.0 42.6 jit_solution(5921774079159635712)
XLA Ops:
  0.6 40.7 %section.1 = (bf16[8,8,2,16,128]{4,3,2,1,0:T(8,128)(2,1)S(1)}, bf16[8,8,2,16,128]{4,3,2,1,0:T(8,128)(2,1)S(1)}, f32[27,8,128]{2,1,0:T(8,128)S(1)}, f32[27,8,128]{2,1,0:T(8,128)S(1)}) custom-call(s32[1,2,2]{2,1,0:T(2,128)} %refs_0_.1, bf16[8,8,2,16,128]{4,3,2,1,0:T(8,128)(2,1)} %bitcast.4, bf16[8,8,2,16,128]{4,3,2,1,0:T(8,128)(2,1)} %bitcast.5, ...), custom_call_target="tpu_custom_call" | custom-call | tf_op jit(solution)/shard_map/section/pallas_call | solution.py:614
  41.4 1.1 %hand_on.1 = (bf16[8,8,2,16,128]{4,3,2,1,0:T(8,128)(2,1)}, bf16[8,8,2,16,128]{4,3,2,1,0:T(8,128)(2,1)}, f32[27,8,128]{2,1,0:T(8,128)}, f32[27,8,128]{2,1,0:T(8,128)}) custom-call(bf16[8,8,2,16,128]{4,3,2,1,0:T(8,128)(2,1)S(1)} %get-tuple-element.12.refs_0_, bf16[8,8,2,16,128]{4,3,2,1,0:T(8,128)(2,1)S(1)} %get-tuple-element.13.refs_1_, ...), custom_call_target="tpu_custom_call" | custom-call | tf_op jit(solution)/shard_map/hand_on/pallas_call | solution.py:625

commit v3 on v2

--- a/solution.py
+++ b/solution.py
@@ -15,6 +15,7 @@
 GX, GY = 8, 16
 X, Y, Z, C = 8, 16, 16, 128
 TAPS = 28
+HALVES = [(0, 4, 0, 8)], [(4, 4, 0, 8)]
 FRONT = [(0, 2, 0, 8)], [(2, 2, 0, 8)]
 BACK = [(4, 2, 0, 8)], [(6, 2, 0, 8)]
 INNER = [(1, 3, 1, 6)], [(4, 3, 1, 6)]
@@ -27,6 +28,11 @@
     (8, FULL, ("y", "x", "z")),
     (16, FULL, ("z", "y", "x")),
     (24, FULL[:3], ("x", "y", "z")),
+)
+
+
+PAIRS = sorted(
+    ((i, j) for i in range(4) for j in range(4) if i or j), key=lambda d: -min(d[0], 4 - d[0]) - min(d[1], 4 - d[1])
 )
 
 
@@ -55,8 +61,8 @@
         ref[n] for n in ("slope", "at", "outs", "part", "r0", "fin", "rfin", "done")
     )
     occ_ref, occ_sem = ref["occ_here"], ref["occ_sem"]
-    in_sem, out_sem, hs, hr, s0s, s0r, rss, rsr, s4s, s4r = (
-        ref[n] for n in ("in_sem", "out_sem", "hs", "hr", "s0s", "s0r", "rss", "rsr", "s4s", "s4r")
+    in_sem, out_sem, hs, hr, sent, s0r, rsr, s4s, s4r = (
+        ref[n] for n in ("in_sem", "out_sem", "hs", "hr", "sent", "s0r", "rsr", "s4s", "s4r")
     )
     gx = lax.axis_index("gx")
     gy = lax.axis_index("gy")
@@ -76,15 +82,9 @@
     def at_z(k):
         return (pz + k) % 4
 
-    def dev_x(k):
-        return (gx, yh * 8 + at_x(k) * 2 + core)
-
-    def dev_y(k):
-        to = at_y(k)
-        return ((to % 2) * 4 + pz, (to // 2) * 8 + px * 2 + core)
-
-    def dev_z(k):
-        return (yl * 4 + at_z(k), gy)
+    def device(x=0, y=0, z=0):
+        to = at_y(y)
+        return ((to % 2) * 4 + at_z(z), (to // 2) * 8 + at_x(x) * 2 + core)
 
     partner = (gx, gy + 1 - 2 * core)
 
@@ -101,26 +101,27 @@
     get_occ.start()
     loads = [
         [
-            pltpu.make_async_copy(src.at[pl.ds(2 * i, 2)], dst.at[pl.ds(2 * i, 2)], in_sem.at[f, i])
+            pltpu.make_async_copy(src.at[pl.ds(2 * i, 2)], dst.at[pl.ds(2 * i, 2)], in_sem.at[4 * f + i])
             for i in range(4)
         ]
         for f, (src, dst) in enumerate(((feat_hbm, feat), (cot_hbm, cot)))
     ]
     loads += [
-        [pltpu.make_async_copy(src, dst, in_sem.at[f, 0])] for f, src, dst in ((2, w1_hbm, w1), (3, w2_hbm, w2))
+        [pltpu.make_async_copy(src, dst, in_sem.at[f])] for f, src, dst in ((8, w1_hbm, w1), (9, w2_hbm, w2))
     ]
     for group in loads:
         for load in group:
             load.start()
     barrier = pltpu.get_barrier_semaphore()
+    fixed = [partner]
+    for axis in "xyz":
+        fixed += [device(**{axis: k}) for k in (1, 2, 3)]
+    for peer in fixed:
+        pl.semaphore_signal(barrier, inc=1, device_id=peer, device_id_type=MESH)
     for ax, ay in DIRS:
         @pl.when(exists(ax, ay))
         def _():
             pl.semaphore_signal(barrier, inc=1, device_id=(gx + ax, gy + ay), device_id_type=MESH)
-    fixed = [partner] + [dev_x(k) for k in (1, 2, 3)] + [dev_y(k) for k in (1, 2, 3)]
-    fixed += [((gx + k) % GX, gy) for k in range(1, GX)]
-    for peer in fixed:
-        pl.semaphore_signal(barrier, inc=1, device_id=peer, device_id_type=MESH)
 
     get_occ.wait()
     low = lax.broadcasted_iota(jnp.int32, (Z, C), 0) < 8
@@ -164,7 +165,7 @@
         return pltpu.make_async_remote_copy(
             src_ref=ref.at[(1, *edge_x(ax, False), *edge_y(ay, False))],
             dst_ref=ref.at[(1, *edge_x(ax, True), *edge_y(ay, True))],
-            send_sem=hs.at[slot, d],
+            send_sem=hs.at[slot % 2, d],
             recv_sem=hr.at[slot, d],
             device_id=(gx + ax, gy + ay),
             device_id_type=MESH,
@@ -217,9 +218,9 @@
 
     zero = jnp.zeros((C, C), BF16)
 
-    def conv(field, w, boxes, flipped):
+    def conv(field, w, boxes, flipped, planes=(0, 1, 2)):
         left, right = [], []
-        for dx in range(3):
+        for dx in planes:
             for dz in range(3):
                 tap = [w[26 - (9 * dx + 3 * dy + dz)] if flipped else w[9 * dx + 3 * dy + dz] for dy in range(3)]
                 for j in range(2):
@@ -274,9 +275,21 @@
             d = jnp.concatenate(d, axis=0) if len(d) > 1 else d[0]
             put(put_padded(hq.at[1]), boxes, grad * d)
 
-    def finish(slot, w, flipped, pair):
-        accs = [conv(hq.at[slot], w, boxes, flipped) for boxes in pair]
+    def begin(slot, w, flipped, plane):
+        sums = [conv(hq.at[slot], w, boxes, flipped, (plane,)) for boxes in HALVES]
+        for total, (box,) in zip(sums, HALVES):
+            x0, nx = box[:2]
+            value = total.reshape(nx, 8, Z, 2 * C)
+            slope[pl.ds(x0, nx)] = value if plane == 0 else slope[pl.ds(x0, nx)] + value
+
+    def finish(slot, w, flipped, pair, planes=(0, 1, 2)):
+        accs = [conv(hq.at[slot], w, boxes, flipped, planes) for boxes in pair]
         base = fu.at[slot]
+        if len(planes) < 3:
+            accs = [
+                acc + slope[pl.ds(x0, nx)].reshape(nx * 8 * Z, 2 * C)
+                for acc, ((x0, nx, _, _),) in zip(accs, pair)
+            ]
 
         def store(x0, nx, k0, nk, h, v):
             b = base[1, pl.ds(x0 + 1, nx), pl.ds(k0 + 1, nk), h].astype(F32)
@@ -328,49 +341,56 @@
         taps = pl.ds(PARTS[p][0], count(p))
         return [
             remote(
-                part.at[g, 1 - core, :, :, taps], r0.at[g, :, :, taps], s0s.at[g, p], s0r.at[g, p], partner
+                part.at[g, 1 - core, :, :, taps], r0.at[g, :, :, taps], sent.at[g, p], s0r.at[g, p], partner
             )
         ]
 
-    def pick(dims, axis, pos):
+    def pick(dims, where):
         index = []
         for d in dims:
-            if d == axis:
-                index.append(pos)
-            elif axis == "y" and d == "yh":
-                index.append(pos // 2)
-            elif axis == "y" and d == "yl":
-                index.append(pos % 2)
+            if d in where:
+                index.append(where[d])
+            elif d == "yh" and "y" in where:
+                index.append(where["y"] // 2)
+            elif d == "yl" and "y" in where:
+                index.append(where["y"] % 2)
             else:
                 index.append(slice(None))
         return tuple(index)
 
-    position = {"x": (at_x, dev_x), "y": (at_y, dev_y), "z": (at_z, dev_z)}
+    position = {"x": at_x, "y": at_y, "z": at_z}
 
     def ring(g, p, stage):
         dims = dims_after(PARTS[p], stage - 1)
-        axis = PARTS[p][2][stage - 1]
-        where, device = position[axis]
-        source = ref[f"h{p}"] if stage == 1 else ref[f"t{p}_{stage - 1}"]
+        axes = PARTS[p][2][:1] if stage == 1 else PARTS[p][2][1:]
+        source = ref[f"h{p}"] if stage == 1 else ref[f"t{p}_1"]
+        steps = [(k,) for k in (2, 1, 3)] if stage == 1 else PAIRS
+        copies = []
+        for n, away in enumerate(steps):
+            where = {axis: position[axis](k) for axis, k in zip(axes, away)}
+            copies.append(
+                remote(
+                    source.at[(g, *pick(dims, where))],
+                    ref[f"r{p}_{stage}"].at[g, n],
+                    sent.at[g, p],
+                    rsr.at[g, p, stage - 1],
+                    device(**dict(zip(axes, away))),
+                )
+            )
+        return copies
+
+    def three(g, p, stage):
+        every = ref[f"r{p}_{stage}"].at[g]
+        return remote(every, every, sent.at[g, p], rsr.at[g, p, stage - 1], partner)
+
+    away = ((2, 1), (2, 0), (1, 1), (3, 1), (1, 0), (3, 0), (0, 1))
+
+    def gather(g):
         return [
             remote(
-                source.at[(g, *pick(dims, axis, where(k)))],
-                ref[f"r{p}_{stage}"].at[g, k - 1],
-                rss.at[g, p, stage - 1],
-                rsr.at[g, p, stage - 1],
-                device(k),
+                fin.at[g], rfin.at[g, i], s4s.at[g], s4r.at[g], ((yl + dy) % 2 * 4 + (pz + dz) % 4, gy)
             )
-            for k in (1, 2, 3)
-        ]
-
-    def three(g, p, stage):
-        every = ref[f"r{p}_{stage}"].at[g]
-        return remote(every, every, rss.at[g, p, stage - 1], rsr.at[g, p, stage - 1], partner)
-
-    def gather(g):
-        return [
-            remote(fin.at[g], rfin.at[g, k - 1], s4s.at[g], s4r.at[g], ((gx + k) % GX, gy))
-            for k in range(1, GX)
+            for i, (dz, dy) in enumerate(away)
         ]
 
     def seven(g):
@@ -392,29 +412,30 @@
             index = (g, slice(None), slice(None)) + ((i // 2, i % 2) if p < 3 else (i,))
             ref[f"t{p}_0"][index] = total
             ref[f"h{p}"][index] = total.astype(BF16)
+        stage0(g, p)[0].wait_send()
         start(ring(g, p, 1))
 
-    def step(g, p, stage):
-        three(g, p, stage).wait_recv()
+    def step(g, p, stage, arrived=False):
+        if not arrived:
+            three(g, p, stage).wait_recv()
         dims = dims_after(PARTS[p], stage - 1)
-        axis = PARTS[p][2][stage - 1]
-        own = ref[f"t{p}_{stage - 1}"][(g, *pick(dims, axis, position[axis][0](0)))]
+        axes = PARTS[p][2][:1] if stage == 1 else PARTS[p][2][1:]
+        own = ref[f"t{p}_{stage - 1}"][(g, *pick(dims, {axis: position[axis](0) for axis in axes}))]
         r = ref[f"r{p}_{stage}"]
-        total = (own + r[g, 0].astype(F32)) + (r[g, 1].astype(F32) + r[g, 2].astype(F32))
-        if stage < 3:
-            ref[f"t{p}_{stage}"][g] = total
-            start(ring(g, p, stage + 1))
+        if stage == 1:
+            total = (own + r[g, 0].astype(F32)) + (r[g, 1].astype(F32) + r[g, 2].astype(F32))
+            ref[f"t{p}_1"][g] = total
+            three(g, p, 1).wait_send()
+            start(ring(g, p, 2))
         else:
-            fin[g, p] = total
+            terms = [own] + [r[g, n] for n in range(len(PAIRS))]
+            while len(terms) > 1:
+                terms = [a + b for a, b in zip(terms[::2], terms[1::2])]
+            fin[g, p] = terms[0]
 
     def settle(g):
         for p in range(4):
-            stage0(g, p)[0].wait_send()
-            three(g, p, 1).wait_send()
             three(g, p, 2).wait_send()
-            if g == 0:
-                three(1, p, 3).wait_send()
-                three(0, p, 3).wait_send()
 
     def spread(g):
         start(gather(g))
@@ -427,14 +448,15 @@
         def _():
             done[g, 24 + pz] = fin[g, 3] * scale
         seven(g).wait_recv()
-        for k in range(1, GX):
-            source = (gx + GX - k) % GX
+        for i, (dz, dy) in enumerate(away):
+            z = (pz + 4 - dz) % 4
+            low_y = (yl + dy) % 2
             for p in range(3):
-                done[g, 8 * p + 2 * (source % 4) + source // 4] = rfin[g, k - 1, p] * scale
-
-            @pl.when(source < 4)
+                done[g, 8 * p + 2 * z + low_y] = rfin[g, i, p] * scale
+
+            @pl.when(low_y == 0)
             def _():
-                done[g, 24 + source] = rfin[g, k - 1, 3] * scale
+                done[g, 24 + z] = rfin[g, i, 3] * scale
         copy = pltpu.make_async_copy(done.at[g, pl.ds(0, 27)], target, out_sem.at[sem])
         copy.start()
         return copy
@@ -466,6 +488,7 @@
     halo_wait(fu.at[0], 0)
     shift_rim(fu.at[0])
     forward(RIM)
+    halo_sent(fu.at[0], 0)
     halo_start(hq.at[0], 2)
     halo_wait(fu.at[1], 1)
     shift_rim(fu.at[1])
@@ -477,9 +500,10 @@
     wgrad(1, 3, fu.at[1], True)
     step0(1, 1)
     backward(RIM)
-    halo_start(hq.at[1], 3)
     step0(1, 2)
     step0(1, 3)
+    halo_sent(fu.at[1], 1)
+    halo_start(hq.at[1], 3)
     turn(hq.at[1])
     wgrad(0, 0, fu.at[0], False)
     wgrad(0, 1, fu.at[0], False)
@@ -490,13 +514,13 @@
     shift_inner(hq.at[0])
     step0(0, 2)
     step0(0, 3)
-    step(1, 0, 1)
-    step(1, 1, 1)
     halo_wait(hq.at[0], 2)
     shift_rim(hq.at[0])
     finish(0, w2, False, FRONT)
-    step(1, 2, 1)
-    step(1, 3, 1)
+    for p in range(4):
+        three(1, p, 1).wait_recv()
+    for p in range(4):
+        step(1, p, 1, True)
     finish(0, w2, False, BACK)
     out_copy = pltpu.make_async_copy(outs.at[0], out_hbm, out_sem.at[0])
     out_copy.start()
@@ -505,34 +529,27 @@
     step(0, 1, 1)
     halo_wait(hq.at[1], 3)
     shift_rim(hq.at[1])
-    finish(1, w1, True, FRONT)
+    begin(1, w1, True, 0)
     step(0, 2, 1)
     step(0, 3, 1)
+    begin(1, w1, True, 1)
     step(1, 0, 2)
     step(1, 1, 2)
     step(1, 2, 2)
     step(1, 3, 2)
-    finish(1, w1, True, BACK)
+    spread(1)
+    finish(1, w1, True, HALVES, (2,))
     gf_copy = pltpu.make_async_copy(outs.at[1], gf_hbm, out_sem.at[1])
     gf_copy.start()
+    settle(1)
     step(0, 0, 2)
     step(0, 1, 2)
     step(0, 2, 2)
     step(0, 3, 2)
-    step(1, 0, 3)
-    step(1, 1, 3)
-    step(1, 2, 3)
-    step(1, 3, 3)
-    spread(1)
-    settle(1)
-    step(0, 0, 3)
-    step(0, 1, 3)
-    step(0, 2, 3)
-    step(0, 3, 3)
     spread(0)
     g2_copy = collect(1, g2_hbm, 2)
-    for slot, field in enumerate((fu.at[0], fu.at[1], hq.at[0], hq.at[1])):
-        halo_sent(field, slot)
+    halo_sent(hq.at[0], 2)
+    halo_sent(hq.at[1], 3)
     settle(0)
     out_copy.wait()
     gf_copy.wait()
@@ -581,25 +598,23 @@
         "done": vm((2, TAPS, *tile), F32),
         "occ_here": pltpu.SMEM((1, 2, 2), jnp.int32),
         "occ_sem": dma((1,)),
-        "in_sem": dma((4, 4)),
+        "in_sem": dma((10,)),
         "out_sem": dma((4,)),
-        "hs": dma((4, 8)),
+        "hs": dma((2, 8)),
         "hr": dma((4, 8)),
-        "s0s": dma((2, 4)),
+        "sent": dma((2, 4)),
         "s0r": dma((2, 4)),
-        "rss": dma((2, 4, 3)),
-        "rsr": dma((2, 4, 3)),
+        "rsr": dma((2, 4, 2)),
         "s4s": dma((2,)),
         "s4r": dma((2,)),
     }
     for p, part in enumerate(PARTS):
         scratch[f"h{p}"] = vm((2, *shape_of(part[1])), BF16)
-        for stage in range(4):
+        for stage in range(2):
             shape = shape_of(dims_after(part, stage))
-            if stage < 3:
-                scratch[f"t{p}_{stage}"] = vm((2, *shape), F32)
-            if stage > 0:
-                scratch[f"r{p}_{stage}"] = vm((2, 3, *shape), BF16 if stage == 1 else F32)
+            scratch[f"t{p}_{stage}"] = vm((2, *shape), F32)
+        scratch[f"r{p}_1"] = vm((2, 3, *shape_of(dims_after(part, 1))), BF16)
+        scratch[f"r{p}_2"] = vm((2, len(PAIRS), *tile), F32)
     names = ("occ", "f_in", "c_in", "w1_in", "w2_in", "out", "gf", "g1", "g2", *scratch)
     shapes = (
         jax.ShapeDtypeStruct(split, BF16),

time: 42.7 us -> 40.3 us (0.944)
  Pallas kernels: 41.8 us -> 39.4 us
    pallas_call x1, Pallas kernels: 40.7 us -> 38.3 us  [body(): pl.pallas_call(functools.partial(kernel, scale, names), name='section', o...]
where the time goes in v3:
time: 40.3 us; the launch traced here: 40.2 us
  Pallas kernels  39.4 us (98%)
  between operations  0.8 us (2%)
    pallas_call x1, Pallas kernels, body(): pl.pallas_call(functools.partial(kernel, scale, names), name='section', o...  38.3 us
    pallas_call x1, Pallas kernels, body(): pl.pallas_call(hand_on, name='hand_on', out_shape=shapes, in_specs=[anysp...  1.06 us

profile of v3, /device:TPU:0, one launch (start us, length us, event | category | flops | bytes accessed | tf_op | source)
XLA Modules:
  0.0 40.2 jit_solution(4977060603791380085)
XLA Ops:
  0.6 38.3 %section.1 = (bf16[8,8,2,16,128]{4,3,2,1,0:T(8,128)(2,1)S(1)}, bf16[8,8,2,16,128]{4,3,2,1,0:T(8,128)(2,1)S(1)}, f32[27,8,128]{2,1,0:T(8,128)S(1)}, f32[27,8,128]{2,1,0:T(8,128)S(1)}) custom-call(s32[1,2,2]{2,1,0:T(2,128)} %refs_0_.1, bf16[8,8,2,16,128]{4,3,2,1,0:T(8,128)(2,1)} %bitcast.4, bf16[8,8,2,16,128]{4,3,2,1,0:T(8,128)(2,1)} %bitcast.5, ...), custom_call_target="tpu_custom_call" | custom-call | tf_op jit(solution)/shard_map/section/pallas_call | solution.py:629
  39.0 1.1 %hand_on.1 = (bf16[8,8,2,16,128]{4,3,2,1,0:T(8,128)(2,1)}, bf16[8,8,2,16,128]{4,3,2,1,0:T(8,128)(2,1)}, f32[27,8,128]{2,1,0:T(8,128)}, f32[27,8,128]{2,1,0:T(8,128)}) custom-call(bf16[8,8,2,16,128]{4,3,2,1,0:T(8,128)(2,1)S(1)} %get-tuple-element.12.refs_0_, bf16[8,8,2,16,128]{4,3,2,1,0:T(8,128)(2,1)S(1)} %get-tuple-element.13.refs_1_, ...), custom_call_target="tpu_custom_call" | custom-call | tf_op jit(solution)/shard_map/hand_on/pallas_call | solution.py:640

commit v4 on v3

--- a/solution.py
+++ b/solution.py
@@ -385,16 +385,24 @@
 
     away = ((2, 1), (2, 0), (1, 1), (3, 1), (1, 0), (3, 0), (0, 1))
 
-    def gather(g):
+    def shares(late):
+        return pl.ds(3, 1) if late else pl.ds(0, 3)
+
+    def gather(g, late):
         return [
             remote(
-                fin.at[g], rfin.at[g, i], s4s.at[g], s4r.at[g], ((yl + dy) % 2 * 4 + (pz + dz) % 4, gy)
+                fin.at[g, shares(late)],
+                rfin.at[g, i, shares(late)],
+                s4s.at[g, late],
+                s4r.at[g, late],
+                ((yl + dy) % 2 * 4 + (pz + dz) % 4, gy),
             )
             for i, (dz, dy) in enumerate(away)
         ]
 
-    def seven(g):
-        return remote(rfin.at[g], rfin.at[g], s4s.at[g], s4r.at[g], partner)
+    def seven(g, late):
+        every = rfin.at[g, :, shares(late)]
+        return remote(every, every, s4s.at[g, late], s4r.at[g, late], partner)
 
     def start(copies):
         for copy in copies:
@@ -437,8 +445,8 @@
         for p in range(4):
             three(g, p, 2).wait_send()
 
-    def spread(g):
-        start(gather(g))
+    def spread(g, late):
+        start(gather(g, late))
 
     def collect(g, target, sem):
         for p in range(3):
@@ -447,7 +455,8 @@
         @pl.when(yl == 0)
         def _():
             done[g, 24 + pz] = fin[g, 3] * scale
-        seven(g).wait_recv()
+        seven(g, 0).wait_recv()
+        seven(g, 1).wait_recv()
         for i, (dz, dy) in enumerate(away):
             z = (pz + 4 - dz) % 4
             low_y = (yl + dy) % 2
@@ -533,20 +542,22 @@
     step(0, 2, 1)
     step(0, 3, 1)
     begin(1, w1, True, 1)
+    finish(1, w1, True, HALVES, (2,))
+    gf_copy = pltpu.make_async_copy(outs.at[1], gf_hbm, out_sem.at[1])
+    gf_copy.start()
     step(1, 0, 2)
     step(1, 1, 2)
     step(1, 2, 2)
+    spread(1, 0)
     step(1, 3, 2)
-    spread(1)
-    finish(1, w1, True, HALVES, (2,))
-    gf_copy = pltpu.make_async_copy(outs.at[1], gf_hbm, out_sem.at[1])
-    gf_copy.start()
+    spread(1, 1)
     settle(1)
     step(0, 0, 2)
     step(0, 1, 2)
     step(0, 2, 2)
+    spread(0, 0)
     step(0, 3, 2)
-    spread(0)
+    spread(0, 1)
     g2_copy = collect(1, g2_hbm, 2)
     halo_sent(hq.at[0], 2)
     halo_sent(hq.at[1], 3)
@@ -556,7 +567,8 @@
     g1_copy = collect(0, g1_hbm, 3)
 
     for g in range(2):
-        seven(g).wait_send()
+        seven(g, 0).wait_send()
+        seven(g, 1).wait_send()
     for copy in (g2_copy, g1_copy):
         copy.wait()
 
@@ -605,8 +617,8 @@
         "sent": dma((2, 4)),
         "s0r": dma((2, 4)),
         "rsr": dma((2, 4, 2)),
-        "s4s": dma((2,)),
-        "s4r": dma((2,)),
+        "s4s": dma((2, 2)),
+        "s4r": dma((2, 2)),
     }
     for p, part in enumerate(PARTS):
         scratch[f"h{p}"] = vm((2, *shape_of(part[1])), BF16)

time: 40.3 us -> 40.2 us (level)
  no operation moved by 1% of the time
where the time goes in v4:
time: 40.2 us; the launch traced here: 40.1 us
  Pallas kernels  39.3 us (98%)
  between operations  0.8 us (2%)
    pallas_call x1, Pallas kernels, body(): pl.pallas_call(functools.partial(kernel, scale, names), name='section', o...  38.2 us
    pallas_call x1, Pallas kernels, body(): pl.pallas_call(hand_on, name='hand_on', out_shape=shapes, in_specs=[anysp...  1.06 us

profile of v4, /device:TPU:0, one launch (start us, length us, event | category | flops | bytes accessed | tf_op | source)
XLA Modules:
  0.0 40.1 jit_solution(15144017323653113684)
XLA Ops:
  0.6 38.2 %section.1 = (bf16[8,8,2,16,128]{4,3,2,1,0:T(8,128)(2,1)S(1)}, bf16[8,8,2,16,128]{4,3,2,1,0:T(8,128)(2,1)S(1)}, f32[27,8,128]{2,1,0:T(8,128)S(1)}, f32[27,8,128]{2,1,0:T(8,128)S(1)}) custom-call(s32[1,2,2]{2,1,0:T(2,128)} %refs_0_.1, bf16[8,8,2,16,128]{4,3,2,1,0:T(8,128)(2,1)} %bitcast.4, bf16[8,8,2,16,128]{4,3,2,1,0:T(8,128)(2,1)} %bitcast.5, ...), custom_call_target="tpu_custom_call" | custom-call | tf_op jit(solution)/shard_map/section/pallas_call | solution.py:641
  38.8 1.1 %hand_on.1 = (bf16[8,8,2,16,128]{4,3,2,1,0:T(8,128)(2,1)}, bf16[8,8,2,16,128]{4,3,2,1,0:T(8,128)(2,1)}, f32[27,8,128]{2,1,0:T(8,128)}, f32[27,8,128]{2,1,0:T(8,128)}) custom-call(bf16[8,8,2,16,128]{4,3,2,1,0:T(8,128)(2,1)S(1)} %get-tuple-element.12.refs_0_, bf16[8,8,2,16,128]{4,3,2,1,0:T(8,128)(2,1)S(1)} %get-tuple-element.13.refs_1_, ...), custom_call_target="tpu_custom_call" | custom-call | tf_op jit(solution)/shard_map/hand_on/pallas_call | solution.py:652
